TPU v7x, 128 devices: a whole 4x4x4 slice. The times are simulated.
128 devices in a mesh: dp: 2 (over core), seq: 4 (over x), tensor: 16 (over y, z).
Axes of the slice: x: 4, y: 4, z: 4, core: 2. Of those that a mesh axis runs over, the one named last changes fastest.
Arguments:
- tokens: bfloat16 [16384, 4096], P(('dp', 'seq', 'tensor')), may hold values from -6 to 6
- cotangent: bfloat16 [16384, 14336], P(('dp', 'seq', 'tensor')), may hold values from -0.046875 to 0.046875
- master: bfloat16 [8, 336, 128, 128], P(None, 'tensor'), as said below
- block_ids: int32 [8, 336], P(None, 'tensor'), may hold values from 0 to 223, as said below
- live_count: int32 [8, 16], P(None, 'tensor'), may hold values from 1 to 21, as said below
Outputs:
- outputs: bfloat16 [16384, 14336], P(('dp', 'seq', 'tensor'))
- w_grad: float32 [8, 336, 128, 128], P(('dp', 'seq'), 'tensor')
Inputs may be any that keep to these rules, and one draw needn't show every extreme that they name: Within each group t the 168 entries block_ids[:, t * 21 : (t + 1) * 21] are distinct. `live_count`: in every group one owner uses all 21 slots. `master`: in every block one entry has the largest magnitude, and no entry of a block, divided by that magnitude over 7, lies within 0.1 of a half-integer.
All inputs are finite; a program needn't handle non-finite values. Where the computation divides by a largest or mean magnitude, that divisor is 1e-20 or more.
Results may differ from a plain program's by a relative error of at most 0.005.
Values may be sent and summed in bfloat16 or wider, within the bound.
A program may use at most 192 MiB of HBM per device.

v0:
```python
import jax
import jax.numpy as jnp
from jax import lax
from jax.sharding import PartitionSpec as P

BS = 128


def fake_quant(master, live_mask):
    master_wide = master.astype(jnp.float32)
    block_peak = jnp.max(jnp.abs(master_wide), axis=(-2, -1), keepdims=True) + 1e-06
    levels = jnp.floor(master_wide * (7.0 / block_peak) + 0.5)
    return (levels * (block_peak / 7.0) * live_mask[..., None, None]).astype(jnp.bfloat16)


def assemble(quantized, slot_ids, row_blocks, col_blocks):
    total_slots = quantized.shape[0]
    block_numbers = jnp.arange(row_blocks * col_blocks, dtype=jnp.int32)
    slot_numbers = jnp.arange(1, total_slots + 1, dtype=jnp.int32)
    matches = (slot_ids[:, None] == block_numbers[None, :]).astype(jnp.int32)
    slot_of_block = jnp.sum(matches * slot_numbers[:, None], axis=0)
    padded = jnp.concatenate([jnp.zeros((1, BS, BS), jnp.bfloat16), quantized], axis=0)
    placed = jnp.take(padded, slot_of_block, axis=0).reshape(row_blocks, col_blocks, BS, BS)
    return placed.transpose(0, 2, 1, 3).reshape(row_blocks * BS, col_blocks * BS)


def dense_gradient(token_rows, grad_rows):
    return lax.dot_general(
        token_rows, grad_rows, (((0,), (0,)), ((), ())), preferred_element_type=jnp.float32
    )


def pick_blocks(full_grad, slot_ids, row_blocks, col_blocks):
    grid_blocks = full_grad.reshape(row_blocks, BS, col_blocks, BS).transpose(0, 2, 1, 3)
    grid_blocks = grid_blocks.reshape(row_blocks * col_blocks, BS, BS)
    return jnp.take(grid_blocks, slot_ids, axis=0)


def shards(tokens, cotangent, master, block_ids, live_count):
    owners, slots = block_ids.shape
    groups = lax.axis_size("tensor")
    live_mask = (jnp.arange(slots, dtype=jnp.int32)[None, :] < live_count).astype(jnp.float32)
    quantized = fake_quant(master, live_mask).reshape(owners * slots, BS, BS)
    slot_ids = block_ids.reshape(owners * slots)
    row_blocks = tokens.shape[1] // BS
    col_blocks = cotangent.shape[1] // (BS * groups)
    dense_weight = assemble(quantized, slot_ids, row_blocks, col_blocks)
    grads_local = lax.all_to_all(cotangent, "tensor", split_axis=1, concat_axis=0, tiled=True)
    gathered = lax.all_gather(tokens, "tensor", axis=0, tiled=True)
    results = jnp.dot(gathered, dense_weight, preferred_element_type=jnp.float32)
    full_grad = dense_gradient(gathered, grads_local)
    outputs = lax.all_to_all(
        results.astype(jnp.bfloat16), "tensor", split_axis=0, concat_axis=1, tiled=True
    )
    partial_value = pick_blocks(full_grad, slot_ids, row_blocks, col_blocks)
    partial_value = (partial_value * live_mask.reshape(owners * slots)[:, None, None]).reshape(
        owners, slots, BS, BS
    )
    w_grad = lax.psum_scatter(partial_value, ("dp", "seq"), scatter_dimension=0, tiled=True)
    return (outputs, w_grad)


def solution(mesh):
    return jax.shard_map(
        shards,
        mesh=mesh,
        in_specs=(
            P(("dp", "seq", "tensor"), None),
            P(("dp", "seq", "tensor"), None),
            P(None, "tensor", None, None),
            P(None, "tensor"),
            P(None, "tensor"),
        ),
        out_specs=(P(("dp", "seq", "tensor"), None), P(("dp", "seq"), "tensor", None, None)),
        check_vma=False,
    )
```

profile of v0, /device:TPU:1, one launch (start us, length us, event | category | flops | bytes accessed | tf_op | source)
XLA Modules:
  0.0 369.7 jit_solution(11243594162319001183)
XLA Ops:
  7.2 0.0 all-gather.2.cloned.1.call-start
  7.2 0.7 all-gather.2.cloned.1.call-update
  7.9 6.1 %copy.33 = bf16[128,14336]{0,1:T(8,128)(2,1)} copy(bf16[128,14336]{1,0:T(8,128)(2,1)} %param.6) | data formatting | bytes 7340032 | tf_op args[1]
  13.9 0.0 copy-start
  14.0 6.1 %copy.34 = bf16[128,16,896]{2,0,1:T(8,128)(2,1)} copy(bf16[128,16,896]{0,2,1:T(8,128)(2,1)} %bitcast.55) | data formatting | bytes 7340032 | tf_op jit(solution)/shard_map/all_to_all | solution.py:48
  20.1 8.6 %all-to-all-start.1 = ((bf16[128,16,896]{2,0,1:T(8,128)(2,1)}), bf16[128,16,896]{2,0,1:T(8,128)(2,1)}, u32[]{:S(2)}, u32[]{:S(2)}) async-start(bf16[128,16,896]{2,0,1:T(8,128)(2,1)} %copy.34), calls=%async_computation.1 | async-start | bytes 7340032 | tf_op jit(solution)/shard_map/all_to_all | solution.py:48
  28.7 0.0 reduce-scatter.2.cloned.1.call-start
  28.8 0.0 copy-done
  28.8 0.1 reshape.139
  28.9 0.0 copy-done.1
  28.9 0.1 fusion.11
  29.0 4.0 %fusion = f32[8,21]{1,0:T(8,128)S(1)} fusion(bf16[8,21,128,128]{3,2,1,0:T(8,128)(2,1)} %param.7), kind=kLoop, calls=%fused_computation.4 | loop fusion | flops 8257368 | bytes 5505696 | tf_op jit(solution)/shard_map/reduce_max | solution.py:11
  32.9 68.2 %all-to-all-done.1 = bf16[128,16,896]{2,0,1:T(8,128)(2,1)} async-done(((bf16[128,16,896]{2,0,1:T(8,128)(2,1)}), bf16[128,16,896]{2,0,1:T(8,128)(2,1)}, u32[]{:S(2)}, u32[]{:S(2)}) %all-to-all-start.1) | async-done | bytes 3670048 | tf_op jit(solution)/shard_map/all_to_all | solution.py:48
  101.2 6.1 %copy.35 = bf16[2048,896]{0,1:T(8,128)(2,1)} copy(bf16[2048,896]{1,0:T(8,128)(2,1)} %bitcast.15) | data formatting | bytes 7340032 | tf_op jit(solution)/shard_map/all_to_all | solution.py:48
  107.2 57.2 %all-gather.2.cloned.1.call-done = bf16[2048,4096]{1,0:T(8,128)(2,1)} async-done(((bf16[128,4096]{1,0:T(8,128)(2,1)}), bf16[2048,4096]{1,0:T(8,128)(2,1)}) %all-gather.2.cloned.1.call-update) | async-done | bytes 16777232 | tf_op jit(solution)/shard_map/all_gather | solution.py:49
  164.5 22.5 %copy.32 = bf16[4096,2048]{1,0:T(8,128)(2,1)} copy(bf16[4096,2048]{0,1:T(8,128)(2,1)} %bitcast.51) | data formatting | bytes 33554432 | tf_op jit(solution)/shard_map/dot_general | solution.py:28
  187.0 23.3 %fusion.12 = f32[32,128,7,128]{3,1,2,0:T(8,128)} fusion(bf16[32,128,2048,1]{2,1,3,0:T(8,128)(2,1)} %bitcast.52, bf16[7,128,2048,1]{2,1,0,3:T(8,128)(2,1)} %bitcast.58), kind=kOutput, calls=%fused_computation.32 | convolution fusion | flops 15032385536 | bytes 35127296 | tf_op jit(solution)/shard_map/dot_general | solution.py:28
  210.3 15.5 %gather_fusion.1 = f32[168,128,128]{2,1,0:T(8,128)} fusion(f32[224,128,128]{2,1,0:T(8,128)} %bitcast.56, s32[1024]{0:T(1024)S(1)} %pad_clamp_fusion), kind=kCustom, calls=%fused_computation.1 | custom fusion | bytes 22020768 | tf_op jit(solution)/shard_map/jit(_take)/gather | solution.py:36
  225.8 14.1 %select_multiply_fusion = (f32[8,21,128,128]{3,2,1,0:T(8,128)}, bf16[8,21,128,128]{3,2,1,0:T(8,128)(2,1)}) fusion(f32[8,21,128,128]{3,2,1,0:T(8,128)} %bitcast.48, f32[8,21]{1,0:T(8,128)S(1)} %get-tuple-element.12, pred[8,21]{1,0:T(8,128)(4,1)S(1)} %get-tuple-element.13, f32[8,21]{1,0:T(8,128)S(1)} %get-tuple-element.11, f32[8,21]{1,0:T(8,128)S(1)} %get-tuple-element.10, ...), kind=kLoop, calls=%fused_computation.10 | loop fusion | flops 24772608 | bytes 33032328 | tf_op jit(solution)/shard_map/mul | solution.py:56
  239.9 0.0 reduce-scatter.2.cloned.1.call-update
  240.0 0.1 eq.15
  240.0 0.1 select_reduce_fusion
  240.2 0.1 reduce_sum.14
  240.3 7.2 %concatenate.3 = bf16[169,128,128]{2,1,0:T(8,128)(2,1)} pad(bf16[168,128,128]{2,1,0:T(8,128)(2,1)} %bitcast.50, bf16[]{:T(256)} %constant.42.clone.1), padding=1_0x0_0x0_0 | pad | bytes 11042818 | tf_op jit(solution)/shard_map/concatenate | solution.py:22
  247.5 11.1 %gather_fusion = bf16[224,128,128]{2,1,0:T(8,128)(2,1)} fusion(bf16[169,128,128]{2,1,0:T(8,128)(2,1)} %concatenate.3, s32[1024]{0:T(1024)S(1)} %pad_clamp_fusion.1), kind=kCustom, calls=%fused_computation | custom fusion | bytes 14680960 | tf_op jit(solution)/shard_map/jit(_take)/gather | solution.py:23
  258.6 6.8 %select_bitcast_fusion = bf16[32,128,7,128]{3,1,2,0:T(8,128)(2,1)} fusion(bf16[32,7,128,128]{3,2,1,0:T(8,128)(2,1)} %bitcast.49, pred[32,7]{1,0:T(8,128)(4,1)S(1)} %compare_and_fusion), kind=kLoop, calls=%fused_computation.14 | loop fusion | flops 3670016 | bytes 14680288 | tf_op jit(solution)/shard_map/transpose | solution.py:24
  265.4 12.2 %copy.30 = bf16[32,128,7,128]{1,0,3,2:T(8,128)(2,1)} copy(bf16[32,128,7,128]{3,1,2,0:T(8,128)(2,1)} %select_bitcast_fusion) | data formatting | bytes 14680064 | tf_op jit(solution)/shard_map/transpose | solution.py:24
  277.6 20.9 %convert_bitcast_fusion = bf16[112,16,8,128]{3,2,1,0:T(8,128)(2,1)S(1)} fusion(bf16[2048,4096]{1,0:T(8,128)(2,1)} %all-gather.2.cloned.1.call-done, bf16[112,8,32,128]{3,2,1,0:T(8,128)(2,1)} %bitcast.57), kind=kOutput, calls=%fused_computation.16 | convolution fusion | flops 15034220544 | bytes 27787264 | tf_op jit(solution)/shard_map/dot_general | solution.py:50
  298.5 0.9 copy.47
  299.5 55.9 %all_to_all.38 = bf16[16,128,896]{1,2,0:T(8,128)(2,1)} all-to-all(bf16[16,128,896]{1,2,0:T(8,128)(2,1)S(1)} %bitcast.53), channel_id=1, replica_groups=mesh['dp'=2,'seq'=4,'tensor'=16] {'tensor'}, dimensions={0} | all-to-all | bytes 7340032 | tf_op jit(solution)/shard_map/all_to_all | solution.py:52
  355.3 6.1 %copy.36 = bf16[128,14336]{1,0:T(8,128)(2,1)} copy(bf16[128,14336]{0,1:T(8,128)(2,1)} %bitcast.54) | data formatting | bytes 7340032
  361.5 1.4 reduce-scatter.2.cloned.1.call-done
  (8 shorter events, 0.0 us)
Async XLA Ops:
  7.2 157.3 %all-gather.2.cloned.1.call-start = ((), (), s32[]{:S(2)}) async-start(), calls=%async_computation.3 | async-start | bytes 17825792 | tf_op jit(solution)/shard_map/all_gather | solution.py:49
  13.9 14.8 %copy-start = (s32[8,21]{1,0:T(8,128)S(1)}, s32[8,21]{1,0:T(8,128)}, u32[]{:S(2)}) copy-start(s32[8,21]{1,0:T(8,128)} %param.8) | copy-start | bytes 2020
  13.9 14.9 %copy-start.1 = (s32[8,1]{0,1:T(1,128)S(1)}, s32[8,1]{0,1:T(1,128)}, u32[]{:S(2)}) copy-start(s32[8,1]{0,1:T(1,128)} %param.9) | copy-start | bytes 100
  20.1 81.1 %all-to-all-start.1 = ((bf16[128,16,896]{2,0,1:T(8,128)(2,1)}), bf16[128,16,896]{2,0,1:T(8,128)(2,1)}, u32[]{:S(2)}, u32[]{:S(2)}) async-start(bf16[128,16,896]{2,0,1:T(8,128)(2,1)} %copy.34), calls=%async_computation.1 | async-start | bytes 7340032 | tf_op jit(solution)/shard_map/all_to_all | solution.py:48
  28.7 334.1 %reduce-scatter.2.cloned.1.call-start = ((), (), s32[]{:S(2)}) async-start(), calls=%async_computation.4 | async-start | bytes 12386304 | tf_op jit(solution)/shard_map/reduce_scatter | solution.py:59
Sparse Core Ops, SparseCore 0:
  10.1 154.2 all-gather.1
  240.1 122.7 reduce-scatter.1
where the time goes:
time: 371 us; the launch traced here: 370 us
  waiting for transfers between devices  128 us (35%)
  local copies, waits for them, and re-layouts  94.1 us (25%)
  blocking collectives  55.9 us (15%)
  matrix products  44.2 us (12%)
  other arithmetic  25.1 us (7%)
  between operations  14.1 us (4%)
  starting transfers between devices  8.72 us (2%)
    all_to_all x1, waiting for transfers between devices, shards(): lax.all_to_all(cotangent, 'tensor', split_axis=1, concat_axis=0, tiled=True)  68.2 us
    all_gather x1, waiting for transfers between devices, shards(): gathered = lax.all_gather(tokens, 'tensor', axis=0, tiled=True)  57.2 us
    all_to_all x1, blocking collectives, shards(): lax.all_to_all(results.astype(jnp.bfloat16), 'tensor', split_axis=0, conc...  55.9 us
    dot_general x1, matrix products, dense_gradient(): lax.dot_general(token_rows, grad_rows, (((0,), (0,)), ((), ())), preferre...  23.3 us
    dot_general x1, local copies, waits for them, and re-layouts, dense_gradient(): lax.dot_general(token_rows, grad_rows, (((0,), (0,)), ((), ())), preferre...  22.5 us
    dot_general x1, matrix products, shards(): jnp.dot(gathered, dense_weight, preferred_element_type=jnp.float32)  20.9 us
    gather x1, local copies, waits for them, and re-layouts, pick_blocks(): return jnp.take(grid_blocks, slot_ids, axis=0)  15.5 us
    mul x1, other arithmetic, shards(): partial_value * live_mask.reshape(owners * slots)[:, None, None]  14.1 us
  transfers between devices with their start and end apart: 3, of which 3 were waited for; matrix products, arithmetic and copies ran while one was open for 24% of the time, Pallas kernels for 0%

commit v1 on v0

--- a/solution.py
+++ b/solution.py
@@ -46,7 +46,9 @@
     col_blocks = cotangent.shape[1] // (BS * groups)
     dense_weight = assemble(quantized, slot_ids, row_blocks, col_blocks)
     grads_local = lax.all_to_all(cotangent, "tensor", split_axis=1, concat_axis=0, tiled=True)
-    gathered = lax.all_gather(tokens, "tensor", axis=0, tiled=True)
+    gathered = jnp.concatenate(
+        lax.all_to_all(jnp.stack([tokens] * lax.axis_size("tensor")), "tensor", 0, 0), axis=0
+    )
     results = jnp.dot(gathered, dense_weight, preferred_element_type=jnp.float32)
     full_grad = dense_gradient(gathered, grads_local)
     outputs = lax.all_to_all(

time: 371 us -> 623 us (1.68)
  waiting for transfers between devices: 128 us -> 346 us
  local copies, waits for them, and re-layouts: 94.1 us -> 122 us
  starting transfers between devices: 8.72 us -> 20.6 us
  blocking collectives: 55.9 us -> 47.8 us
    all_to_all x0 -> x1, waiting for transfers between devices: none -> 285 us  [shards(): lax.all_to_all(jnp.stack([tokens] * lax.axis_size('tensor')), 'tensor', 0...]
    all_gather x1 -> x0, waiting for transfers between devices: 57.2 us -> none  [shards(): gathered = lax.all_gather(tokens, 'tensor', axis=0, tiled=True)]
    all_to_all x0 -> x1, local copies, waits for them, and re-layouts: none -> 21.4 us  [shards(): lax.all_to_all(jnp.stack([tokens] * lax.axis_size('tensor')), 'tensor', 0...]
    all_to_all x1, waiting for transfers between devices: 68.2 us -> 48.5 us  [shards(): lax.all_to_all(cotangent, 'tensor', split_axis=1, concat_axis=0, tiled=True)]
    all_to_all x0 -> x1, starting transfers between devices: none -> 11.9 us  [shards(): lax.all_to_all(jnp.stack([tokens] * lax.axis_size('tensor')), 'tensor', 0...]
    reduce_scatter x1, waiting for transfers between devices: 1.39 us -> 12.4 us  [shards(): lax.psum_scatter(partial_value, ('dp', 'seq'), scatter_dimension=0, tiled...]
    all_to_all x1, blocking collectives: 55.9 us -> 47.8 us  [shards(): lax.all_to_all(results.astype(jnp.bfloat16), 'tensor', split_axis=0, conc...]
    unnamed x6 -> x9, local copies, waits for them, and re-layouts: 12.2 us -> 12.8 us
  transfers between devices with their start and end apart: 3 -> 3, of which waited for: 3 -> 3; matrix products, arithmetic and copies ran while one was open for 24% -> 12% of each run, Pallas kernels for 0% -> 0%
where the time goes in v1:
time: 623 us; the launch traced here: 621 us
  waiting for transfers between devices  346 us (56%)
  local copies, waits for them, and re-layouts  122 us (20%)
  blocking collectives  47.8 us (8%)
  matrix products  44.2 us (7%)
  other arithmetic  25.6 us (4%)
  starting transfers between devices  20.6 us (3%)
  between operations  14.1 us (2%)
    all_to_all x1, waiting for transfers between devices, shards(): lax.all_to_all(jnp.stack([tokens] * lax.axis_size('tensor')), 'tensor', 0...  285 us
    all_to_all x1, waiting for transfers between devices, shards(): lax.all_to_all(cotangent, 'tensor', split_axis=1, concat_axis=0, tiled=True)  48.5 us
    all_to_all x1, blocking collectives, shards(): lax.all_to_all(results.astype(jnp.bfloat16), 'tensor', split_axis=0, conc...  47.8 us
    dot_general x1, matrix products, dense_gradient(): lax.dot_general(token_rows, grad_rows, (((0,), (0,)), ((), ())), preferre...  23.3 us
    dot_general x1, local copies, waits for them, and re-layouts, dense_gradient(): lax.dot_general(token_rows, grad_rows, (((0,), (0,)), ((), ())), preferre...  22.5 us
    all_to_all x1, local copies, waits for them, and re-layouts, shards(): lax.all_to_all(jnp.stack([tokens] * lax.axis_size('tensor')), 'tensor', 0...  21.4 us
    dot_general x1, matrix products, shards(): jnp.dot(gathered, dense_weight, preferred_element_type=jnp.float32)  20.9 us
    gather x1, local copies, waits for them, and re-layouts, pick_blocks(): return jnp.take(grid_blocks, slot_ids, axis=0)  15.5 us
  transfers between devices with their start and end apart: 3, of which 3 were waited for; matrix products, arithmetic and copies ran while one was open for 12% of the time, Pallas kernels for 0%

profile of v1, /device:TPU:1, one launch (start us, length us, event | category | flops | bytes accessed | tf_op | source)
XLA Modules:
  0.0 620.9 jit_solution(14415822602403579232)
XLA Ops:
  7.2 6.1 copy.37
  13.2 6.2 copy.38
  19.4 8.6 %all-to-all-start.2 = ((bf16[128,16,896]{2,0,1:T(8,128)(2,1)}), bf16[128,16,896]{2,0,1:T(8,128)(2,1)}, u32[]{:S(2)}, u32[]{:S(2)}) async-start(bf16[128,16,896]{2,0,1:T(8,128)(2,1)} %copy.38), calls=%async_computation.2 | async-start | bytes 7340032 | tf_op jit(solution)/shard_map/all_to_all | solution.py:48
  28.0 0.0 copy-done
  28.1 0.7 copy.33
  28.7 48.5 %all-to-all-done.2 = bf16[128,16,896]{2,0,1:T(8,128)(2,1)} async-done(((bf16[128,16,896]{2,0,1:T(8,128)(2,1)}), bf16[128,16,896]{2,0,1:T(8,128)(2,1)}, u32[]{:S(2)}, u32[]{:S(2)}) %all-to-all-start.2) | async-done | bytes 3670048 | tf_op jit(solution)/shard_map/all_to_all | solution.py:48
  77.3 6.1 stack.2
  83.3 11.9 %all-to-all-start = ((bf16[16,128,4096]{1,2,0:T(8,128)(2,1)}), bf16[16,128,4096]{1,2,0:T(8,128)(2,1)}, u32[]{:S(2)}, u32[]{:S(2)}) async-start(bf16[16,128,4096]{1,2,0:T(8,128)(2,1)} %stack.2), calls=%async_computation | async-start | bytes 33554432 | tf_op jit(solution)/shard_map/all_to_all | solution.py:50
  95.2 0.0 reduce-scatter.2.cloned.1.call-start
  95.3 0.1 reshape.145
  95.4 0.1 fusion.11
  95.5 3.9 fusion
  99.4 6.1 copy.39
  105.4 285.3 %all-to-all-done = bf16[16,128,4096]{1,2,0:T(8,128)(2,1)} async-done(((bf16[16,128,4096]{1,2,0:T(8,128)(2,1)}), bf16[16,128,4096]{1,2,0:T(8,128)(2,1)}, u32[]{:S(2)}, u32[]{:S(2)}) %all-to-all-start) | async-done | bytes 16777248 | tf_op jit(solution)/shard_map/all_to_all | solution.py:50
  390.7 21.4 %copy.34 = bf16[16,128,4096]{2,1,0:T(8,128)(2,1)} copy(bf16[16,128,4096]{1,2,0:T(8,128)(2,1)} %all-to-all-done) | data formatting | bytes 33554432 | tf_op jit(solution)/shard_map/all_to_all | solution.py:50
  412.2 22.5 %copy.36 = bf16[4096,2048]{1,0:T(8,128)(2,1)} copy(bf16[4096,2048]{0,1:T(8,128)(2,1)} %bitcast.50) | data formatting | bytes 33554432 | tf_op jit(solution)/shard_map/dot_general | solution.py:28
  434.7 23.3 %fusion.12 = f32[32,128,7,128]{3,1,2,0:T(8,128)} fusion(bf16[32,128,2048,1]{2,1,3,0:T(8,128)(2,1)} %bitcast.55, bf16[7,128,2048,1]{2,1,0,3:T(8,128)(2,1)} %bitcast.61), kind=kOutput, calls=%fused_computation.32 | convolution fusion | flops 15032385536 | bytes 35127296 | tf_op jit(solution)/shard_map/dot_general | solution.py:28
  458.0 15.5 %gather_fusion.1 = f32[168,128,128]{2,1,0:T(8,128)} fusion(f32[224,128,128]{2,1,0:T(8,128)} %bitcast.59, s32[1024]{0:T(1024)S(1)} %pad_clamp_fusion), kind=kCustom, calls=%fused_computation.1 | custom fusion | bytes 22020768 | tf_op jit(solution)/shard_map/jit(_take)/gather | solution.py:36
  473.5 14.1 %select_multiply_fusion = (f32[8,21,128,128]{3,2,1,0:T(8,128)}, bf16[8,21,128,128]{3,2,1,0:T(8,128)(2,1)}) fusion(f32[8,21,128,128]{3,2,1,0:T(8,128)} %bitcast.52, f32[8,21]{1,0:T(8,128)S(1)} %get-tuple-element.12, pred[8,21]{1,0:T(8,128)(4,1)S(1)} %get-tuple-element.13, f32[8,21]{1,0:T(8,128)S(1)} %get-tuple-element.11, f32[8,21]{1,0:T(8,128)S(1)} %get-tuple-element.10, ...), kind=kLoop, calls=%fused_computation.10 | loop fusion | flops 24772608 | bytes 33032328 | tf_op jit(solution)/shard_map/mul | solution.py:58
  487.6 0.0 reduce-scatter.2.cloned.1.call-update
  487.6 0.1 eq.15
  487.7 0.1 select_reduce_fusion
  487.8 0.1 reduce_sum.14
  488.0 7.2 %concatenate.3 = bf16[169,128,128]{2,1,0:T(8,128)(2,1)} pad(bf16[168,128,128]{2,1,0:T(8,128)(2,1)} %bitcast.54, bf16[]{:T(256)} %constant.42.clone.1), padding=1_0x0_0x0_0 | pad | bytes 11042818 | tf_op jit(solution)/shard_map/concatenate | solution.py:22
  495.2 11.1 %gather_fusion = bf16[224,128,128]{2,1,0:T(8,128)(2,1)} fusion(bf16[169,128,128]{2,1,0:T(8,128)(2,1)} %concatenate.3, s32[1024]{0:T(1024)S(1)} %pad_clamp_fusion.1), kind=kCustom, calls=%fused_computation | custom fusion | bytes 14680960 | tf_op jit(solution)/shard_map/jit(_take)/gather | solution.py:23
  506.3 7.3 %select_bitcast_fusion = bf16[32,128,7,128]{3,1,2,0:T(8,128)(2,1)} fusion(bf16[32,7,128,128]{3,2,1,0:T(8,128)(2,1)} %bitcast.53, pred[32,7]{1,0:T(8,128)(4,1)S(1)} %compare_and_fusion), kind=kLoop, calls=%fused_computation.14 | loop fusion | flops 3670016 | bytes 14680288 | tf_op jit(solution)/shard_map/transpose | solution.py:24
  513.6 12.1 %copy.32 = bf16[32,128,7,128]{1,0,3,2:T(8,128)(2,1)} copy(bf16[32,128,7,128]{3,1,2,0:T(8,128)(2,1)} %select_bitcast_fusion) | data formatting | bytes 14680064 | tf_op jit(solution)/shard_map/transpose | solution.py:24
  525.8 20.9 %convert_bitcast_fusion = bf16[112,16,8,128]{3,2,1,0:T(8,128)(2,1)S(1)} fusion(bf16[2048,4096]{1,0:T(8,128)(2,1)} %bitcast.51, bf16[112,8,32,128]{3,2,1,0:T(8,128)(2,1)} %bitcast.60), kind=kOutput, calls=%fused_computation.16 | convolution fusion | flops 15034220544 | bytes 27787264 | tf_op jit(solution)/shard_map/dot_general | solution.py:52
  546.7 0.9 copy.51
  547.7 47.8 %all_to_all.43 = bf16[16,128,896]{1,2,0:T(8,128)(2,1)} all-to-all(bf16[16,128,896]{1,2,0:T(8,128)(2,1)S(1)} %bitcast.56), channel_id=1, replica_groups=mesh['dp'=2,'seq'=4,'tensor'=16] {'tensor'}, dimensions={0} | all-to-all | bytes 7340032 | tf_op jit(solution)/shard_map/all_to_all | solution.py:54
  595.5 6.1 copy.40
  601.6 12.4 %reduce-scatter.2.cloned.1.call-done = f32[1,21,128,128]{3,2,1,0:T(8,128)} async-done(((f32[8,21,128,128]{3,2,1,0:T(8,128)}), f32[1,21,128,128]{3,2,1,0:T(8,128)}) %reduce-scatter.2.cloned.1.call-update) | async-done | bytes 1376272 | tf_op jit(solution)/shard_map/reduce_scatter | solution.py:61
  (12 shorter events, 0.1 us)
Async XLA Ops:
  13.2 14.8 %copy-start = (bf16[128,4096]{1,0:T(8,128)(2,1)S(1)}, bf16[128,4096]{1,0:T(8,128)(2,1)}, u32[]{:S(2)}) copy-start(bf16[128,4096]{1,0:T(8,128)(2,1)} %param.5) | copy-start | bytes 3145732
  19.4 57.9 %all-to-all-start.2 = ((bf16[128,16,896]{2,0,1:T(8,128)(2,1)}), bf16[128,16,896]{2,0,1:T(8,128)(2,1)}, u32[]{:S(2)}, u32[]{:S(2)}) async-start(bf16[128,16,896]{2,0,1:T(8,128)(2,1)} %copy.38), calls=%async_computation.2 | async-start | bytes 7340032 | tf_op jit(solution)/shard_map/all_to_all | solution.py:48
  83.3 11.9 %copy-start.1 = (s32[8,21]{1,0:T(8,128)S(1)}, s32[8,21]{1,0:T(8,128)}, u32[]{:S(2)}) copy-start(s32[8,21]{1,0:T(8,128)} %param.8) | copy-start | bytes 2020
  83.3 12.1 %copy-start.2 = (s32[8,1]{0,1:T(1,128)S(1)}, s32[8,1]{0,1:T(1,128)}, u32[]{:S(2)}) copy-start(s32[8,1]{0,1:T(1,128)} %param.9) | copy-start | bytes 100
  83.3 307.4 %all-to-all-start = ((bf16[16,128,4096]{1,2,0:T(8,128)(2,1)}), bf16[16,128,4096]{1,2,0:T(8,128)(2,1)}, u32[]{:S(2)}, u32[]{:S(2)}) async-start(bf16[16,128,4096]{1,2,0:T(8,128)(2,1)} %stack.2), calls=%async_computation | async-start | bytes 33554432 | tf_op jit(solution)/shard_map/all_to_all | solution.py:50
  95.2 518.8 %reduce-scatter.2.cloned.1.call-start = ((), (), s32[]{:S(2)}) async-start(), calls=%async_computation.4 | async-start | bytes 12386304 | tf_op jit(solution)/shard_map/reduce_scatter | solution.py:61
Sparse Core Ops, SparseCore 0:
  487.8 126.2 reduce-scatter.1
